TPU v7x, 512 devices: a whole 4x8x8 slice. The times are simulated.
512 devices in a mesh: req: 64 (over x, y, core), tp: 8 (over z).
Axes of the slice: x: 4, y: 8, z: 8, core: 2. Of those that a mesh axis runs over, the one named last changes fastest.
Arguments:
- queries: bfloat16 [64, 28, 4096], P('req', None, 'tp'), may hold values from -25 to 25
- tree_kv: bfloat16 [64, 28, 2048], P('req', None, 'tp'), may hold values from -4 to 4
- tree_parent: int32 [64, 28], P('req'), may hold values from -1 to 26, as said below
- accepted_path: int32 [64, 8], replicated, may hold values from -1 to 27, as said below
- cache_kv: bfloat16 [192, 256, 2048], P('req', None, 'tp'), may hold values from -6 to 6
- piece_owner: int32 [192, 2], P('req'), may hold values from -1 to 63, as said below
- cache_len: int32 [64], replicated, may hold values from 1 to 1016, as said below
- out_weight: bfloat16 [4096, 4096], P('tp', 'req'), may hold values from -0.09375 to 0.09375
Outputs:
- mixed: bfloat16 [64, 28, 4096], P('tp', None, 'req')
- cache_out: bfloat16 [192, 256, 2048], P('req', None, 'tp')
Inputs may be any that keep to these rules, and one draw needn't show every extreme that they name: tree_parent[r, 0] = -1 and 0 <= tree_parent[r, i] < i for i >= 1; tokens 1 to 7 have parent i - 1. accepted_path[r] lists, root first, the tokens on the path from token 0 to some token of request r's tree, then -1 entries; it holds 1 to 8 tokens, and 8 for some request. piece_owner[s] = (r, p) means slot s holds cache rows p * 256 to p * 256 + 255 of request r; (-1, -1) marks an unused slot. For each request r the pieces 0 to (cache_len[r] + 7) // 256 stand in exactly one slot each, and no other pieces do. cache_len[r] + 8 <= 1024.
All inputs are finite; a program needn't handle non-finite values.
Results may differ from a plain program's by a relative error of at most 0.02.
Values may be sent and summed in bfloat16 or wider, within the bound.
No kernel may reach another device: no remote copies, remote signals or barrier semaphores. Data moves between devices by JAX's collectives and lax.ppermute only.
A program may use at most 64 MiB of HBM per device.

v0:
```python
import math
import jax
import jax.numpy as jnp
from jax import lax
from jax.sharding import PartitionSpec as P

HD = 128
NEG = -1e30


def ancestors(parent):
    tree_size = parent.shape[-1]
    node_ids = lax.broadcasted_iota(jnp.int32, (tree_size, tree_size), 1)
    parent_hot = (parent[..., :, None] == node_ids).astype(jnp.float32)
    reached = jnp.minimum(parent_hot + jnp.eye(tree_size, dtype=jnp.float32), 1.0)
    for rounds in range(max(1, (tree_size - 1).bit_length())):
        reached = jnp.minimum(
            jnp.einsum("rij,rjk->rik", reached, reached, precision=lax.Precision.HIGHEST), 1.0
        )
    return reached


def shards(
    queries, tree_kv, tree_parent, accepted_path, cache_kv, piece_owner, cache_len, out_weight
):
    kvheads_local = tree_kv.shape[-1] // (2 * HD)
    heads_local = queries.shape[-1] // HD
    group_size = heads_local // kvheads_local
    tree_size = queries.shape[1]
    slot_count = cache_kv.shape[0]
    piece_rows = cache_kv.shape[1]
    depth_most = accepted_path.shape[1]
    scaling = 1.0 / math.sqrt(HD)
    every_query = lax.all_gather(queries, "req", axis=0, tiled=True)
    req_total = every_query.shape[0]
    owner_req = piece_owner[:, 0]
    owner_piece = piece_owner[:, 1]
    safe_req = jnp.maximum(owner_req, 0)
    slot_query = every_query[safe_req].reshape(slot_count, tree_size, kvheads_local, group_size, HD)
    stored = cache_kv.reshape(slot_count, piece_rows, kvheads_local, 2, HD)
    row_pos = owner_piece[:, None] * piece_rows + lax.broadcasted_iota(
        jnp.int32, (slot_count, piece_rows), 1
    )
    visible = (owner_req >= 0)[:, None] & (row_pos < cache_len[safe_req][:, None])
    wide_mask = visible[:, None, None, None, :]
    scores = (
        jnp.einsum(
            "stkgd,spkd->stkgp", slot_query, stored[:, :, :, 0], preferred_element_type=jnp.float32
        )
        * scaling
    )
    scores = jnp.where(wide_mask, scores, NEG)
    slot_peak = jnp.max(scores, -1)
    expo = jnp.where(wide_mask, jnp.exp(scores - slot_peak[..., None]), 0.0)
    slot_den = jnp.sum(expo, -1)
    weights = expo.astype(jnp.bfloat16)
    slot_num = jnp.einsum(
        "stkgp,spkd->stkgd", weights, stored[:, :, :, 1], preferred_element_type=jnp.float32
    )
    request_ids = lax.broadcasted_iota(jnp.int32, (req_total, slot_count), 0)
    member = (owner_req[None, :] == request_ids)[:, :, None, None, None]
    req_peak = jnp.max(jnp.where(member, slot_peak[None], NEG), axis=1)
    factor = jnp.where(
        member, jnp.exp(jnp.where(member, slot_peak[None] - req_peak[:, None], 0.0)), 0.0
    )
    req_den = jnp.sum(factor * slot_den[None], axis=1)
    req_num = jnp.einsum("rstkg,stkgd->rtkgd", factor, slot_num, precision=lax.Precision.HIGHEST)
    peak_table = req_peak.reshape(req_total, tree_size, heads_local)
    den_table = req_den.reshape(req_total, tree_size, heads_local)
    num_table = req_num.reshape(req_total, tree_size, heads_local * HD)
    own_index = lax.axis_index("req")
    got_peak, got_den, got_num = (
        lax.all_to_all(
            peak_table.astype(jnp.bfloat16), "req", split_axis=0, concat_axis=0, tiled=True
        ).astype(peak_table.dtype),
        lax.all_to_all(
            den_table.astype(jnp.bfloat16), "req", split_axis=0, concat_axis=0, tiled=True
        ).astype(den_table.dtype),
        lax.all_to_all(
            num_table.astype(jnp.bfloat16), "req", split_axis=0, concat_axis=0, tiled=True
        ).astype(num_table.dtype),
    )
    cache_peak = jnp.max(got_peak, axis=0)
    source_scale = jnp.exp(got_peak - cache_peak[None])
    cache_den = jnp.sum(source_scale * got_den, axis=0)
    got_rows = got_num.reshape(got_num.shape[0], tree_size, heads_local, HD)
    cache_num = jnp.sum(source_scale[..., None] * got_rows, axis=0)
    reached = ancestors(tree_parent)[0]
    home_query = queries[0].reshape(tree_size, kvheads_local, group_size, HD)
    fresh = tree_kv[0].reshape(tree_size, kvheads_local, 2, HD)
    tree_mask = reached[:, None, None, :] > 0.5
    tree_scores = (
        jnp.einsum("ikgd,jkd->ikgj", home_query, fresh[:, :, 0], preferred_element_type=jnp.float32)
        * scaling
    )
    tree_scores = jnp.where(tree_mask, tree_scores, NEG)
    tree_peak = jnp.max(tree_scores, -1)
    tree_exp = jnp.where(tree_mask, jnp.exp(tree_scores - tree_peak[..., None]), 0.0)
    tree_den = jnp.sum(tree_exp, -1).reshape(tree_size, heads_local)
    tree_num = jnp.einsum(
        "ikgj,jkd->ikgd",
        tree_exp.astype(jnp.bfloat16),
        fresh[:, :, 1],
        preferred_element_type=jnp.float32,
    )
    tree_num = tree_num.reshape(tree_size, heads_local, HD)
    tree_peak = tree_peak.reshape(tree_size, heads_local)
    total_peak = jnp.maximum(cache_peak, tree_peak)
    cache_scale = jnp.exp(cache_peak - total_peak)
    tree_scale = jnp.exp(tree_peak - total_peak)
    denom = cache_den * cache_scale + tree_den * tree_scale
    numer = cache_num * cache_scale[..., None] + tree_num * tree_scale[..., None]
    attention = (
        (numer / denom[..., None]).reshape(1, tree_size, heads_local * HD).astype(jnp.bfloat16)
    )
    piece = lax.all_gather(attention, "req", axis=0, tiled=True)
    flat_rows = piece.reshape(piece.shape[0] * piece.shape[1], piece.shape[2])
    product = jnp.dot(flat_rows, out_weight, preferred_element_type=jnp.float32)
    terms = product.reshape(piece.shape[0], piece.shape[1], out_weight.shape[1])
    mixed = lax.psum_scatter(terms.astype(jnp.bfloat16), "tp", scatter_dimension=0, tiled=True)
    own_path = lax.dynamic_index_in_dim(accepted_path, own_index, 0, keepdims=False)
    picked = tree_kv[0][jnp.maximum(own_path, 0)]
    picked = jnp.where((own_path >= 0)[:, None], picked, jnp.zeros_like(picked))
    all_rows = lax.all_gather(picked[None], "req", axis=0, tiled=True)
    counts = jnp.sum((accepted_path >= 0).astype(jnp.int32), axis=1)
    offset = row_pos - cache_len[safe_req][:, None]
    writing = (owner_req >= 0)[:, None] & (offset >= 0) & (offset < counts[safe_req][:, None])
    slot_rows = all_rows[safe_req]
    chosen = jnp.take_along_axis(slot_rows, jnp.clip(offset, 0, depth_most - 1)[:, :, None], axis=1)
    cache_out = jnp.where(writing[:, :, None], chosen, cache_kv)
    return (mixed, cache_out)


def solution(mesh):
    return jax.shard_map(
        shards,
        mesh=mesh,
        in_specs=(
            P("req", None, "tp"),
            P("req", None, "tp"),
            P("req", None),
            P(),
            P("req", None, "tp"),
            P("req", None),
            P(),
            P("tp", "req"),
        ),
        out_specs=(P("tp", None, "req"), P("req", None, "tp")),
        check_vma=False,
    )
```

profile of v0, /device:TPU:2, one launch (start us, length us, event | category | flops | bytes accessed | tf_op | source)
XLA Modules:
  0.0 331.0 jit_solution(16705288890588195445)
XLA Ops:
  7.9 1.2 copy.126
  11.2 1.3 gather_fusion
  13.3 84.3 %all-gather.3.cloned.1.call-done = bf16[64,28,512]{2,1,0:T(8,128)(2,1)} async-done(((bf16[1,28,512]{2,1,0:T(8,128)(2,1)}), bf16[64,28,512]{2,1,0:T(8,128)(2,1)}) %all-gather.3.cloned.1.call-update) | async-done | bytes 1835024 | tf_op jit(solution)/shard_map/all_gather | solution.py:34
  97.6 2.1 gather_fusion.1
  100.9 0.8 copy.130
  101.7 8.0 %all-to-all-start = ((bf16[64,28,4]{1,2,0:T(4,128)(2,1)}), bf16[64,28,4]{1,2,0:T(4,128)(2,1)S(1)}, u32[]{:S(2)}, u32[]{:S(2)}) async-start(bf16[64,28,4]{1,2,0:T(4,128)(2,1)} %copy.130), calls=%async_computation | async-start | bytes 131072 | tf_op jit(solution)/shard_map/all_to_all | solution.py:73
  110.9 7.5 %all-to-all-done = bf16[64,28,4]{1,2,0:T(4,128)(2,1)S(1)} async-done(((bf16[64,28,4]{1,2,0:T(4,128)(2,1)}), bf16[64,28,4]{1,2,0:T(4,128)(2,1)S(1)}, u32[]{:S(2)}, u32[]{:S(2)}) %all-to-all-start) | async-done | bytes 14368 | tf_op jit(solution)/shard_map/all_to_all | solution.py:73
  118.5 5.5 %all-to-all-start.2 = ((bf16[64,28,4]{1,2,0:T(4,128)(2,1)}), bf16[64,28,4]{1,2,0:T(4,128)(2,1)S(1)}, u32[]{:S(2)}, u32[]{:S(2)}) async-start(bf16[64,28,4]{1,2,0:T(4,128)(2,1)} %copy.151), calls=%async_computation.2 | async-start | bytes 131072 | tf_op jit(solution)/shard_map/all_to_all | solution.py:76
  124.0 6.0 %convert_bitcast_fusion = bf16[64,28,1,4,128]{4,0,3,1,2:T(8,128)(2,1)S(1)} fusion(f32[3,28,4,128]{3,1,2,0:T(8,128)S(1)} %fusion.19, f32[64,28,4]{0,2,1:T(4,128)S(1)} %select_reduce_fusion, f32[3,28,4]{0,2,1:T(4,128)S(1)} %copy.137, pred[64,3]{0,1:T(4,128)(4,1)S(1)} %iota_compare_fusion), kind=kOutput, calls=%fused_computation.9 | convolution fusion | flops 34012160 | bytes 2037248 | tf_op jit(solution)/shard_map/rstkg,stkgd->rtkgd/dot_general | solution.py:67
  130.0 1.4 copy.161
  131.4 1.8 reshape.676
  133.3 10.7 %all-to-all-start.1 = ((bf16[64,28,512]{2,1,0:T(8,128)(2,1)}), bf16[64,28,512]{2,1,0:T(8,128)(2,1)S(1)}, u32[]{:S(2)}, u32[]{:S(2)}) async-start(bf16[64,28,512]{2,1,0:T(8,128)(2,1)} %reshape.676), calls=%async_computation.1 | async-start | bytes 4194304 | tf_op jit(solution)/shard_map/all_to_all | solution.py:79
  147.0 3.5 %mul.113 = f32[64,28,4,128]{3,2,0,1:T(4,128)} broadcast(f32[64,28,4]{2,0,1:T(8,128)S(1)} %copy.135), dimensions={0,1,2} | broadcast | bytes 3698688 | tf_op jit(solution)/shard_map/mul | solution.py:87
  150.5 5.2 %mul.114 = f32[64,28,512]{2,0,1:T(8,128)} reshape(f32[64,28,4,128]{3,2,0,1:T(4,128)} %mul.113) | data formatting | bytes 7340032 | tf_op jit(solution)/shard_map/mul | solution.py:87
  155.7 37.8 %all-to-all-done.1 = bf16[64,28,512]{2,1,0:T(8,128)(2,1)S(1)} async-done(((bf16[64,28,512]{2,1,0:T(8,128)(2,1)}), bf16[64,28,512]{2,1,0:T(8,128)(2,1)S(1)}, u32[]{:S(2)}, u32[]{:S(2)}) %all-to-all-start.1) | async-done | bytes 1835040 | tf_op jit(solution)/shard_map/all_to_all | solution.py:79
  193.5 3.6 %multiply_reduce_fusion = f32[28,512]{1,0:T(8,128)S(1)} fusion(f32[64,28,512]{2,0,1:T(8,128)} %mul.114, bf16[64,28,512]{2,1,0:T(8,128)(2,1)S(1)} %all-to-all-done.1), kind=kLoop, calls=%fused_computation.6 | loop fusion | flops 2738176 | bytes 5562368 | tf_op jit(solution)/shard_map/reduce_sum | solution.py:87
  199.2 37.4 %all_gather.11 = bf16[64,8,256]{2,1,0:T(8,128)(2,1)S(1)} all-gather(bf16[1,8,256]{2,1,0:T(8,128)(2,1)S(1)} %bitcast_select_fusion), channel_id=1, replica_groups=mesh['req'=64,'tp'=8] {'req'}, dimensions={0}, use_global_device_ids=true | all-gather | bytes 266240 | tf_op jit(solution)/shard_map/all_gather | solution.py:124
  237.2 41.2 %all-gather.5.cloned.1.call-done = bf16[64,28,512]{2,1,0:T(8,128)(2,1)} async-done(((bf16[1,28,512]{2,1,0:T(8,128)(2,1)}), bf16[64,28,512]{2,1,0:T(8,128)(2,1)}) %all-gather.5.cloned.1.call-update) | async-done | bytes 1835024 | tf_op jit(solution)/shard_map/all_gather | solution.py:116
  278.4 3.7 %fusion.2 = bf16[64,28,64]{2,0,1:T(8,128)(2,1)S(1)} fusion(bf16[64,28,512]{2,1,0:T(8,128)(2,1)} %all-gather.5.cloned.1.call-done, bf16[512,64]{0,1:T(8,128)(2,1)S(1)} %copy-done), kind=kOutput, calls=%fused_computation.10 | convolution fusion | flops 117555200 | bytes 2129920 | tf_op jit(solution)/shard_map/dot_general | solution.py:118
  282.4 1.1 reshape.677
  283.7 4.2 %gather_fusion.5 = bf16[768,256]{1,0:T(8,128)(2,1)S(1)} fusion(bf16[3,8,256]{2,1,0:T(8,128)(2,1)S(1)} %gather_fusion.4, s32[768]{0:T(1024)S(1)} %reshape.664), kind=kCustom, calls=%fused_computation.5 | custom fusion | bytes 792576 | tf_op jit(solution)/shard_map/jit(take_along_axis)/gather | solution.py:129
  287.9 1.0 select_select_fusion
  288.9 34.0 %reduce-scatter.4.cloned.1.call-done = bf16[8,1792]{1,0:T(8,128)(2,1)} async-done(((bf16[64,1792]{1,0:T(8,128)(2,1)}), bf16[8,1792]{1,0:T(8,128)(2,1)}) %reduce-scatter.4.cloned.1.call-update) | async-done | bytes 28688
  322.9 0.9 reshape.678
  (77 shorter events, 12.7 us)
Async XLA Ops:
  7.2 271.3 %copy-start = (bf16[512,64]{0,1:T(8,128)(2,1)S(1)}, bf16[512,64]{0,1:T(8,128)(2,1)}, u32[]{:S(2)}) copy-start(bf16[512,64]{0,1:T(8,128)(2,1)} %param.15) | copy-start | bytes 196612
  7.2 90.4 %all-gather.3.cloned.1.call-start = ((), (), s32[]{:S(2)}) async-start(), calls=%async_computation.4 | async-start | bytes 2129920 | tf_op jit(solution)/shard_map/all_gather | solution.py:34
  101.7 16.8 %all-to-all-start = ((bf16[64,28,4]{1,2,0:T(4,128)(2,1)}), bf16[64,28,4]{1,2,0:T(4,128)(2,1)S(1)}, u32[]{:S(2)}, u32[]{:S(2)}) async-start(bf16[64,28,4]{1,2,0:T(4,128)(2,1)} %copy.130), calls=%async_computation | async-start | bytes 131072 | tf_op jit(solution)/shard_map/all_to_all | solution.py:73
  118.5 14.8 %all-to-all-start.2 = ((bf16[64,28,4]{1,2,0:T(4,128)(2,1)}), bf16[64,28,4]{1,2,0:T(4,128)(2,1)S(1)}, u32[]{:S(2)}, u32[]{:S(2)}) async-start(bf16[64,28,4]{1,2,0:T(4,128)(2,1)} %copy.151), calls=%async_computation.2 | async-start | bytes 131072 | tf_op jit(solution)/shard_map/all_to_all | solution.py:76
  133.3 10.7 %copy-start.3 = (bf16[1,28,512]{2,1,0:T(8,128)(2,1)S(1)}, bf16[1,28,512]{2,1,0:T(8,128)(2,1)}, u32[]{:S(2)}) copy-start(bf16[1,28,512]{2,1,0:T(8,128)(2,1)} %param.8) | copy-start | bytes 86020
  133.3 10.8 %copy-start.2 = (bf16[1,28,256]{2,1,0:T(8,128)(2,1)S(1)}, bf16[1,28,256]{2,1,0:T(8,128)(2,1)}, u32[]{:S(2)}) copy-start(bf16[1,28,256]{2,1,0:T(8,128)(2,1)} %param.9) | copy-start | bytes 43012
  133.3 10.8 %copy-start.5 = (s32[1,28]{1,0:T(1,128)S(1)}, s32[1,28]{1,0:T(1,128)}, u32[]{:S(2)}) copy-start(s32[1,28]{1,0:T(1,128)} %param.10) | copy-start | bytes 340
  133.3 60.2 %all-to-all-start.1 = ((bf16[64,28,512]{2,1,0:T(8,128)(2,1)}), bf16[64,28,512]{2,1,0:T(8,128)(2,1)S(1)}, u32[]{:S(2)}, u32[]{:S(2)}) async-start(bf16[64,28,512]{2,1,0:T(8,128)(2,1)} %reshape.676), calls=%async_computation.1 | async-start | bytes 4194304 | tf_op jit(solution)/shard_map/all_to_all | solution.py:79
  143.9 134.5 %all-gather.5.cloned.1.call-start = ((), (), s32[]{:S(2)}) async-start(), calls=%async_computation.5 | async-start | bytes 2129920 | tf_op jit(solution)/shard_map/all_gather | solution.py:116
  155.7 42.5 %copy-start.4 = (s32[64,8]{0,1:T(8,128)S(1)}, s32[64,8]{0,1:T(8,128)}, u32[]{:S(2)}) copy-start(s32[64,8]{0,1:T(8,128)} %param.11) | copy-start | bytes 6148
  198.1 124.8 %reduce-scatter.4.cloned.1.call-start = ((), (), s32[]{:S(2)}) async-start(), calls=%async_computation.6 | async-start | bytes 258048
  283.6 4.3 %copy-start.1 = (bf16[3,256,256]{2,1,0:T(8,128)(2,1)S(1)}, bf16[3,256,256]{2,1,0:T(8,128)(2,1)}, u32[]{:S(2)}) copy-start(bf16[3,256,256]{2,1,0:T(8,128)(2,1)} %param.12) | copy-start | bytes 1179652
Sparse Core Ops, SparseCore 0:
  11.4 86.1 all-gather.2
  198.3 80.1 all-gather.4
  283.7 39.1 reduce-scatter.3
where the time goes:
time: 332 us; the launch traced here: 331 us
  waiting for transfers between devices  206 us (62%)
  blocking collectives  37.4 us (11%)
  local copies, waits for them, and re-layouts  29.6 us (9%)
  starting transfers between devices  24.3 us (7%)
  between operations  14.1 us (4%)
  matrix products  11.4 us (3%)
  other arithmetic  8.73 us (3%)
    all_gather x1, waiting for transfers between devices, shards(): every_query = lax.all_gather(queries, 'req', axis=0, tiled=True)  84.3 us
    all_gather x1, waiting for transfers between devices, shards(): piece = lax.all_gather(attention, 'req', axis=0, tiled=True)  41.2 us
    all_to_all x1, waiting for transfers between devices, shards(): lax.all_to_all(num_table.astype(jnp.bfloat16), 'req', split_axis=0, conca...  37.8 us
    all_gather x1, blocking collectives, shards(): all_rows = lax.all_gather(picked[None], 'req', axis=0, tiled=True)  37.4 us
    unnamed x4, waiting for transfers between devices  34.7 us
    all_to_all x1, starting transfers between devices, shards(): lax.all_to_all(num_table.astype(jnp.bfloat16), 'req', split_axis=0, conca...  10.7 us
    mul x2, local copies, waits for them, and re-layouts, shards(): cache_num = jnp.sum(source_scale[..., None] * got_rows, axis=0)  8.76 us
    all_to_all x1, starting transfers between devices, shards(): lax.all_to_all(peak_table.astype(jnp.bfloat16), 'req', split_axis=0, conc...  7.97 us
  transfers between devices with their start and end apart: 6, of which 5 were waited for; matrix products, arithmetic and copies ran while one was open for 10% of the time, Pallas kernels for 0%

commit v1 on v0

--- a/solution.py
+++ b/solution.py
@@ -6,6 +6,11 @@
 
 HD = 128
 NEG = -1e30
+
+
+def exchange_gather(x, name, dim):
+    outgoing = jnp.stack([x] * lax.axis_size(name))
+    return jnp.concatenate(lax.all_to_all(outgoing, name, 0, 0), axis=dim)
 
 
 def ancestors(parent):
@@ -31,7 +36,7 @@
     piece_rows = cache_kv.shape[1]
     depth_most = accepted_path.shape[1]
     scaling = 1.0 / math.sqrt(HD)
-    every_query = lax.all_gather(queries, "req", axis=0, tiled=True)
+    every_query = exchange_gather(queries, "req", 0)
     req_total = every_query.shape[0]
     owner_req = piece_owner[:, 0]
     owner_piece = piece_owner[:, 1]

time: 332 us -> 305 us (0.919)
  waiting for transfers between devices: 206 us -> 167 us
  starting transfers between devices: 24.3 us -> 34.6 us
    all_gather x1 -> x0, waiting for transfers between devices: 84.3 us -> none  [shards(): every_query = lax.all_gather(queries, 'req', axis=0, tiled=True)]
    all_to_all x0 -> x1, waiting for transfers between devices: none -> 47.2 us  [exchange_gather(): return jnp.concatenate(lax.all_to_all(outgoing, name, 0, 0), axis=dim)]
    all_to_all x0 -> x1, starting transfers between devices: none -> 10.8 us  [exchange_gather(): return jnp.concatenate(lax.all_to_all(outgoing, name, 0, 0), axis=dim)]
    all_to_all x1, waiting for transfers between devices: 37.8 us -> 34.4 us  [shards(): lax.all_to_all(num_table.astype(jnp.bfloat16), 'req', split_axis=0, conca...]
    unnamed x4 -> x3, waiting for transfers between devices: 34.7 us -> 34 us
  transfers between devices with their start and end apart: 6 -> 6, of which waited for: 5 -> 5; matrix products, arithmetic and copies ran while one was open for 10% -> 11% of each run, Pallas kernels for 0% -> 0%
where the time goes in v1:
time: 305 us; the launch traced here: 304 us
  waiting for transfers between devices  167 us (55%)
  blocking collectives  37.4 us (12%)
  starting transfers between devices  34.6 us (11%)
  local copies, waits for them, and re-layouts  31.4 us (10%)
  between operations  14.5 us (5%)
  matrix products  11.3 us (4%)
  other arithmetic  7.49 us (2%)
    all_to_all x1, waiting for transfers between devices, exchange_gather(): return jnp.concatenate(lax.all_to_all(outgoing, name, 0, 0), axis=dim)  47.2 us
    all_gather x1, waiting for transfers between devices, shards(): piece = lax.all_gather(attention, 'req', axis=0, tiled=True)  44.1 us
    all_gather x1, blocking collectives, shards(): all_rows = lax.all_gather(picked[None], 'req', axis=0, tiled=True)  37.4 us
    all_to_all x1, waiting for transfers between devices, shards(): lax.all_to_all(num_table.astype(jnp.bfloat16), 'req', split_axis=0, conca...  34.4 us
    unnamed x3, waiting for transfers between devices  34 us
    all_to_all x1, starting transfers between devices, exchange_gather(): return jnp.concatenate(lax.all_to_all(outgoing, name, 0, 0), axis=dim)  10.8 us
    all_to_all x1, starting transfers between devices, shards(): lax.all_to_all(num_table.astype(jnp.bfloat16), 'req', split_axis=0, conca...  10.5 us
    mul x2, local copies, waits for them, and re-layouts, shards(): cache_num = jnp.sum(source_scale[..., None] * got_rows, axis=0)  8.76 us
  transfers between devices with their start and end apart: 6, of which 5 were waited for; matrix products, arithmetic and copies ran while one was open for 11% of the time, Pallas kernels for 0%

profile of v1, /device:TPU:2, one launch (start us, length us, event | category | flops | bytes accessed | tf_op | source)
XLA Modules:
  0.0 304.1 jit_solution(11283914893103346649)
XLA Ops:
  7.2 2.4 stack.2
  9.6 10.8 %all-to-all-start = ((bf16[64,1,28,512]{3,2,1,0:T(8,128)(2,1)}), bf16[64,1,28,512]{3,2,1,0:T(8,128)(2,1)S(1)}, u32[]{:S(2)}, u32[]{:S(2)}) async-start(bf16[64,1,28,512]{3,2,1,0:T(8,128)(2,1)} %stack.2), calls=%async_computation | async-start | bytes 4194304 | tf_op jit(solution)/shard_map/all_to_all | solution.py:13
  22.7 47.2 %all-to-all-done = bf16[64,1,28,512]{3,2,1,0:T(8,128)(2,1)S(1)} async-done(((bf16[64,1,28,512]{3,2,1,0:T(8,128)(2,1)}), bf16[64,1,28,512]{3,2,1,0:T(8,128)(2,1)S(1)}, u32[]{:S(2)}, u32[]{:S(2)}) %all-to-all-start) | async-done | bytes 1835040 | tf_op jit(solution)/shard_map/all_to_all | solution.py:13
  71.7 0.8 copy.129
  72.4 7.5 %all-to-all-start.1 = ((bf16[64,28,4]{1,2,0:T(4,128)(2,1)}), bf16[64,28,4]{1,2,0:T(4,128)(2,1)S(1)}, u32[]{:S(2)}, u32[]{:S(2)}) async-start(bf16[64,28,4]{1,2,0:T(4,128)(2,1)} %copy.129), calls=%async_computation.1 | async-start | bytes 131072 | tf_op jit(solution)/shard_map/all_to_all | solution.py:78
  81.2 7.5 %all-to-all-done.1 = bf16[64,28,4]{1,2,0:T(4,128)(2,1)S(1)} async-done(((bf16[64,28,4]{1,2,0:T(4,128)(2,1)}), bf16[64,28,4]{1,2,0:T(4,128)(2,1)S(1)}, u32[]{:S(2)}, u32[]{:S(2)}) %all-to-all-start.1) | async-done | bytes 14368 | tf_op jit(solution)/shard_map/all_to_all | solution.py:78
  88.8 5.5 %all-to-all-start.3 = ((bf16[64,28,4]{1,2,0:T(4,128)(2,1)}), bf16[64,28,4]{1,2,0:T(4,128)(2,1)S(1)}, u32[]{:S(2)}, u32[]{:S(2)}) async-start(bf16[64,28,4]{1,2,0:T(4,128)(2,1)} %copy.150), calls=%async_computation.3 | async-start | bytes 131072 | tf_op jit(solution)/shard_map/all_to_all | solution.py:81
  94.3 6.0 %convert_bitcast_fusion = bf16[64,28,1,4,128]{4,0,3,1,2:T(8,128)(2,1)S(1)} fusion(f32[3,28,4,128]{3,1,2,0:T(8,128)S(1)} %fusion.19, f32[64,28,4]{0,2,1:T(4,128)S(1)} %select_reduce_fusion, f32[3,28,4]{0,2,1:T(4,128)S(1)} %copy.136, pred[64,3]{0,1:T(4,128)(4,1)S(1)} %iota_compare_fusion), kind=kOutput, calls=%fused_computation.9 | convolution fusion | flops 34012160 | bytes 2037248 | tf_op jit(solution)/shard_map/rstkg,stkgd->rtkgd/dot_general | solution.py:72
  100.3 1.4 copy.160
  101.7 1.8 reshape.683
  103.6 10.5 %all-to-all-start.2 = ((bf16[64,28,512]{2,1,0:T(8,128)(2,1)}), bf16[64,28,512]{2,1,0:T(8,128)(2,1)S(1)}, u32[]{:S(2)}, u32[]{:S(2)}) async-start(bf16[64,28,512]{2,1,0:T(8,128)(2,1)} %reshape.683), calls=%async_computation.2 | async-start | bytes 4194304 | tf_op jit(solution)/shard_map/all_to_all | solution.py:84
  119.2 1.2 copy.134
  120.4 3.5 %mul.113 = f32[64,28,4,128]{3,2,0,1:T(4,128)} broadcast(f32[64,28,4]{2,0,1:T(8,128)S(1)} %copy.134), dimensions={0,1,2} | broadcast | bytes 3698688 | tf_op jit(solution)/shard_map/mul | solution.py:92
  124.0 5.2 %mul.114 = f32[64,28,512]{2,0,1:T(8,128)} reshape(f32[64,28,4,128]{3,2,0,1:T(4,128)} %mul.113) | data formatting | bytes 7340032 | tf_op jit(solution)/shard_map/mul | solution.py:92
  129.2 34.4 %all-to-all-done.2 = bf16[64,28,512]{2,1,0:T(8,128)(2,1)S(1)} async-done(((bf16[64,28,512]{2,1,0:T(8,128)(2,1)}), bf16[64,28,512]{2,1,0:T(8,128)(2,1)S(1)}, u32[]{:S(2)}, u32[]{:S(2)}) %all-to-all-start.2) | async-done | bytes 1835040 | tf_op jit(solution)/shard_map/all_to_all | solution.py:84
  163.6 3.3 %multiply_reduce_fusion = f32[28,512]{1,0:T(8,128)S(1)} fusion(f32[64,28,512]{2,0,1:T(8,128)} %mul.114, bf16[64,28,512]{2,1,0:T(8,128)(2,1)S(1)} %all-to-all-done.2), kind=kLoop, calls=%fused_computation.6 | loop fusion | flops 2738176 | bytes 5562368 | tf_op jit(solution)/shard_map/reduce_sum | solution.py:92
  169.1 37.4 %all_gather.7 = bf16[64,8,256]{2,1,0:T(8,128)(2,1)S(1)} all-gather(bf16[1,8,256]{2,1,0:T(8,128)(2,1)S(1)} %bitcast_select_fusion), channel_id=1, replica_groups=mesh['req'=64,'tp'=8] {'req'}, dimensions={0}, use_global_device_ids=true | all-gather | bytes 266240 | tf_op jit(solution)/shard_map/all_gather | solution.py:129
  207.1 44.1 %all-gather.2.cloned.1.call-done = bf16[64,28,512]{2,1,0:T(8,128)(2,1)} async-done(((bf16[1,28,512]{2,1,0:T(8,128)(2,1)}), bf16[64,28,512]{2,1,0:T(8,128)(2,1)}) %all-gather.2.cloned.1.call-update) | async-done | bytes 1835024 | tf_op jit(solution)/shard_map/all_gather | solution.py:121
  251.2 3.7 %fusion.2 = bf16[64,28,64]{2,0,1:T(8,128)(2,1)S(1)} fusion(bf16[64,28,512]{2,1,0:T(8,128)(2,1)} %all-gather.2.cloned.1.call-done, bf16[512,64]{0,1:T(8,128)(2,1)S(1)} %copy-done), kind=kOutput, calls=%fused_computation.10 | convolution fusion | flops 117555200 | bytes 2129920 | tf_op jit(solution)/shard_map/dot_general | solution.py:123
  255.3 1.1 reshape.684
  256.5 4.2 %gather_fusion.5 = bf16[768,256]{1,0:T(8,128)(2,1)S(1)} fusion(bf16[3,8,256]{2,1,0:T(8,128)(2,1)S(1)} %gather_fusion.4, s32[768]{0:T(1024)S(1)} %reshape.671), kind=kCustom, calls=%fused_computation.5 | custom fusion | bytes 792576 | tf_op jit(solution)/shard_map/jit(take_along_axis)/gather | solution.py:134
  260.7 1.0 select_select_fusion
  261.8 34.0 %reduce-scatter.4.cloned.1.call-done = bf16[8,1792]{1,0:T(8,128)(2,1)} async-done(((bf16[64,1792]{1,0:T(8,128)(2,1)}), bf16[8,1792]{1,0:T(8,128)(2,1)}) %reduce-scatter.4.cloned.1.call-update) | async-done | bytes 28688
  295.7 0.9 reshape.685
  (99 shorter events, 14.0 us)
Async XLA Ops:
  7.2 244.1 %copy-start = (bf16[512,64]{0,1:T(8,128)(2,1)S(1)}, bf16[512,64]{0,1:T(8,128)(2,1)}, u32[]{:S(2)}) copy-start(bf16[512,64]{0,1:T(8,128)(2,1)} %param.15) | copy-start | bytes 196612
  9.6 10.8 %copy-start.2 = (bf16[3,256,256]{2,1,0:T(8,128)(2,1)S(1)}, bf16[3,256,256]{2,1,0:T(8,128)(2,1)}, u32[]{:S(2)}) copy-start(bf16[3,256,256]{2,1,0:T(8,128)(2,1)} %param.12) | copy-start | bytes 1179652
  9.6 11.0 %copy-start.15 = (s32[3,2]{0,1:T(2,128)S(1)}, s32[3,2]{0,1:T(2,128)}, u32[]{:S(2)}) copy-start(s32[3,2]{0,1:T(2,128)} %param.13) | copy-start | bytes 76
  9.6 11.1 %copy-start.8 = (s32[64,8]{0,1:T(8,128)S(1)}, s32[64,8]{0,1:T(8,128)}, u32[]{:S(2)}) copy-start(s32[64,8]{0,1:T(8,128)} %param.11) | copy-start | bytes 6148
  9.6 11.7 %copy-start.1 = (s32[64]{0:T(128)S(1)}, s32[64]{0:T(128)}, u32[]{:S(2)}) copy-start(s32[64]{0:T(128)} %param.14) | copy-start | bytes 772
  9.6 60.3 %all-to-all-start = ((bf16[64,1,28,512]{3,2,1,0:T(8,128)(2,1)}), bf16[64,1,28,512]{3,2,1,0:T(8,128)(2,1)S(1)}, u32[]{:S(2)}, u32[]{:S(2)}) async-start(bf16[64,1,28,512]{3,2,1,0:T(8,128)(2,1)} %stack.2), calls=%async_computation | async-start | bytes 4194304 | tf_op jit(solution)/shard_map/all_to_all | solution.py:13
  20.6 50.3 %copy-start.9 = (s32[3]{0:T(128)}, s32[3]{0:T(128)S(1)}, u32[]{:S(2)}) copy-start(s32[3]{0:T(128)S(1)} %get-tuple-element.14) | copy-start | bytes 40
  21.9 48.6 %copy-start.11 = (s32[3]{0:T(128)}, s32[3]{0:T(128)S(1)}, u32[]{:S(2)}) copy-start(s32[3]{0:T(128)S(1)} %gather_fusion) | copy-start | bytes 40
  72.4 16.4 %all-to-all-start.1 = ((bf16[64,28,4]{1,2,0:T(4,128)(2,1)}), bf16[64,28,4]{1,2,0:T(4,128)(2,1)S(1)}, u32[]{:S(2)}, u32[]{:S(2)}) async-start(bf16[64,28,4]{1,2,0:T(4,128)(2,1)} %copy.129), calls=%async_computation.1 | async-start | bytes 131072 | tf_op jit(solution)/shard_map/all_to_all | solution.py:78
  88.8 14.8 %all-to-all-start.3 = ((bf16[64,28,4]{1,2,0:T(4,128)(2,1)}), bf16[64,28,4]{1,2,0:T(4,128)(2,1)S(1)}, u32[]{:S(2)}, u32[]{:S(2)}) async-start(bf16[64,28,4]{1,2,0:T(4,128)(2,1)} %copy.150), calls=%async_computation.3 | async-start | bytes 131072 | tf_op jit(solution)/shard_map/all_to_all | solution.py:81
  103.6 10.8 %copy-start.4 = (bf16[1,28,512]{2,1,0:T(8,128)(2,1)S(1)}, bf16[1,28,512]{2,1,0:T(8,128)(2,1)}, u32[]{:S(2)}) copy-start(bf16[1,28,512]{2,1,0:T(8,128)(2,1)} %param.8) | copy-start | bytes 86020
  103.6 10.8 %copy-start.3 = (bf16[1,28,256]{2,1,0:T(8,128)(2,1)S(1)}, bf16[1,28,256]{2,1,0:T(8,128)(2,1)}, u32[]{:S(2)}) copy-start(bf16[1,28,256]{2,1,0:T(8,128)(2,1)} %param.9) | copy-start | bytes 43012
  103.6 10.8 %copy-start.16 = (s32[1,28]{1,0:T(1,128)S(1)}, s32[1,28]{1,0:T(1,128)}, u32[]{:S(2)}) copy-start(s32[1,28]{1,0:T(1,128)} %param.10) | copy-start | bytes 340
  103.6 60.0 %all-to-all-start.2 = ((bf16[64,28,512]{2,1,0:T(8,128)(2,1)}), bf16[64,28,512]{2,1,0:T(8,128)(2,1)S(1)}, u32[]{:S(2)}, u32[]{:S(2)}) async-start(bf16[64,28,512]{2,1,0:T(8,128)(2,1)} %reshape.683), calls=%async_computation.2 | async-start | bytes 4194304 | tf_op jit(solution)/shard_map/all_to_all | solution.py:84
  114.1 137.2 %all-gather.2.cloned.1.call-start = ((), (), s32[]{:S(2)}) async-start(), calls=%async_computation.5 | async-start | bytes 2129920 | tf_op jit(solution)/shard_map/all_gather | solution.py:121
  129.2 37.7 %copy-start.5 = (f32[28,4]{1,0:T(8,128)S(1)}, f32[28,4]{1,0:T(8,128)}, u32[]{:S(2)}) copy-start(f32[28,4]{1,0:T(8,128)} %copy.154) | copy-start | bytes 1348
  129.2 37.8 %copy-start.6 = (f32[28,4]{1,0:T(8,128)S(1)}, f32[28,4]{1,0:T(8,128)}, u32[]{:S(2)}) copy-start(f32[28,4]{1,0:T(8,128)} %copy.148) | copy-start | bytes 1348
  129.2 37.9 %copy-start.7 = (f32[28,4]{1,0:T(8,128)S(1)}, f32[28,4]{1,0:T(8,128)}, u32[]{:S(2)}) copy-start(f32[28,4]{1,0:T(8,128)} %copy.144) | copy-start | bytes 1348
  168.0 127.7 %reduce-scatter.4.cloned.1.call-start = ((), (), s32[]{:S(2)}) async-start(), calls=%async_computation.6 | async-start | bytes 258048
  207.1 49.3 %copy-start.10 = (s32[3]{0:T(128)S(1)}, s32[3]{0:T(128)}, u32[]{:S(2)}) copy-start(s32[3]{0:T(128)} %copy-done.9) | copy-start | bytes 40
  207.1 49.3 %copy-start.12 = (s32[3]{0:T(128)S(1)}, s32[3]{0:T(128)}, u32[]{:S(2)}) copy-start(s32[3]{0:T(128)} %copy-done.11) | copy-start | bytes 40
  256.4 4.3 %copy-start.13 = (pred[3,256]{1,0:T(4,128)(4,1)S(1)}, pred[3,256]{1,0:T(4,128)(4,1)}, u32[]{:S(2)}) copy-start(pred[3,256]{1,0:T(4,128)(4,1)} %get-tuple-element.9) | copy-start | bytes 2308
  256.4 4.4 %copy-start.14 = (pred[3,256]{1,0:T(4,128)(4,1)S(1)}, pred[3,256]{1,0:T(4,128)(4,1)}, u32[]{:S(2)}) copy-start(pred[3,256]{1,0:T(4,128)(4,1)} %get-tuple-element.11) | copy-start | bytes 2308
Sparse Core Ops, SparseCore 0:
  168.1 83.0 all-gather.1
  256.5 39.1 reduce-scatter.3
